TPU v7x, 512 devices: a whole 4x4x16 slice. The times are simulated.
512 devices in a mesh: chan: 32 (over y, z_lo, core), freq: 16 (over z_hi, x).
Axes of the slice: x: 4, y: 4, z: 16 (z_hi: 4, z_lo: 4; z = z_hi * 4 + z_lo), core: 2. Of those that a mesh axis runs over, the one named last changes fastest.
Arguments:
- spectra: bfloat16 [2, 30, 1024, 4096], P(None, None, 'freq', 'chan'), may hold values from -6 to 6
- src_ids: int32 [2, 32], replicated, may hold values from 0 to 4095
- pair_bin: int32 [2, 32, 4096], P(None, None, 'chan'), may hold values from 0 to 1023, as said below
- slot_of_bin: int32 [1024], replicated, may hold values from 0 to 1023, each once
Outputs:
- offset_gather: float32 [1024, 256], P('chan')
Inputs may be any that keep to these rules, and one draw needn't show every extreme that they name: slot_of_bin names every row of offset_gather once. `pair_bin`: some offset bins are named by no pair.
All inputs are finite; a program needn't handle non-finite values.
Results may differ from a plain program's by a relative error of at most 0.0003.
Values may be sent and summed in bfloat16 or wider, within the bound.
A program may use at most 64 MiB of HBM per device.

v0:
```python
import math
import jax
import jax.numpy as jnp
from jax import lax
from jax.sharding import PartitionSpec as P

F = 1024
NLAG = 256


def lag_basis(anchor, amount, totals, lag_count, windows):
    frequency = anchor + lax.iota(jnp.int32, amount)
    shifts = lax.iota(jnp.int32, lag_count) - lag_count // 2
    phases = frequency[:, None] * shifts[None, :] % (2 * totals)
    angles = phases.astype(jnp.float32) * (math.pi / totals)
    factor = 1.0 / math.sqrt(windows * totals)
    return jnp.concatenate([jnp.cos(angles), -jnp.sin(angles)], axis=0) * factor


def picked(spectra, wanted):
    chans = spectra.shape[3]
    chan_ids = lax.axis_index("chan") * chans + lax.iota(jnp.int32, chans)
    picker = (chan_ids[:, None] == wanted[None, :]).astype(spectra.dtype)
    return jnp.einsum("kwfc,cs->kwfs", spectra, picker, preferred_element_type=jnp.float32)


def cross_terms(source, spectra):
    flipped = jnp.stack([-source[1], source[0]])
    stacked = jnp.stack([source, flipped])
    crossed = jnp.einsum("jkwfs,kwfc->scjf", stacked, spectra, preferred_element_type=jnp.float32)
    return crossed.reshape(source.shape[3] * spectra.shape[3], 2 * spectra.shape[2])


def body(spectra, src_ids, pair_bin, slot_of_bin):
    windows = spectra.shape[1]
    freq_dev = spectra.shape[2]
    steps = pair_bin.shape[0]
    bin_total = slot_of_bin.shape[0]
    lag_table = lag_basis(lax.axis_index("freq") * freq_dev, freq_dev, F, NLAG, windows)
    counts = jnp.zeros((bin_total,), jnp.float32)
    summed = jnp.zeros((bin_total, NLAG), jnp.float32)
    for step_no in range(steps):
        source = lax.psum(picked(spectra, src_ids[step_no]).astype(jnp.bfloat16), "chan")
        crossed = cross_terms(source, spectra)
        bin_ids = pair_bin[step_no].reshape(-1)
        counts = counts + jax.ops.segment_sum(
            jnp.ones((bin_ids.shape[0],), jnp.float32), bin_ids, num_segments=bin_total
        )
        traces = jnp.dot(crossed, lag_table, precision=lax.Precision.HIGHEST)
        summed = summed + jax.ops.segment_sum(traces, bin_ids, num_segments=bin_total)
    summed = jax.ops.segment_sum(summed, slot_of_bin, num_segments=bin_total)
    counts = jax.ops.segment_sum(counts, slot_of_bin, num_segments=bin_total)
    owned, owned_counts = (
        lax.psum_scatter(summed, "chan", scatter_dimension=0, tiled=True),
        lax.psum_scatter(counts, "chan", scatter_dimension=0, tiled=True),
    )
    totals = lax.psum(owned, "freq")
    return totals / jnp.sqrt(jnp.maximum(owned_counts, 1.0))[:, None]


def solution(mesh):
    return jax.shard_map(
        body,
        mesh=mesh,
        in_specs=(P(None, None, "freq", "chan"), P(), P(None, None, "chan"), P()),
        out_specs=P("chan", None),
        check_vma=False,
    )
```

profile of v0, /device:TPU:128, one launch (start us, length us, event | category | flops | bytes accessed | tf_op | source)
XLA Modules:
  0.0 636.5 jit_solution(4346508088757996681)
XLA Ops:
  6.5 0.0 copy-start
  6.5 0.0 copy-start.4
  6.5 0.0 all-reduce.4.cloned.1.call-start
  6.5 0.8 slice_bitcast_fusion.2
  7.3 0.4 copy-done
  7.8 1.8 fusion.6
  9.6 1.8 fusion.7
  11.4 0.0 all-reduce.4.cloned.1.call-update
  11.4 0.0 reduce-scatter.2.cloned.1.call-start
  11.5 0.0 copy-done.4
  11.5 0.3 fusion.22
  11.9 288.8 %all-reduce.4.cloned.1.call-done = (bf16[2,30,64,32]{2,3,1,0:T(8,128)(2,1)}, bf16[2,30,64,32]{2,3,1,0:T(8,128)(2,1)}) async-done(((bf16[2,30,64,32]{2,3,1,0:T(8,128)(2,1)}, bf16[2,30,64,32]{2,3,1,0:T(8,128)(2,1)}), (bf16[2,30,64,32]{2,3,1,0:T(8,128)(2,1)}, bf16[2,30,64,32]{2,3,1,0:T(8,128)(2,1)})) %all-reduce.4.cloned.1.call-update) | async-done | bytes 491536 | tf_op jit(solution)/shard_map/psum | solution.py:43
  300.6 0.0 copy-start.2
  300.6 2.1 slice_negate_fusion
  302.8 0.1 maximum_bitcast_fusion
  302.9 0.0 copy-done.2
  302.9 1.2 pad_maximum_fusion
  304.1 4.5 copy.15
  308.6 1.2 convolution_bitcast_fusion.1
  309.7 0.0 copy-start.3
  309.7 0.0 copy-start.1
  309.7 0.2 copy.17
  309.9 0.7 copy-done.3
  310.7 0.1 maximum_bitcast_fusion.1
  310.8 0.1 copy-done.1
  310.9 1.2 pad_maximum_fusion.1
  312.1 5.3 copy.18
  317.4 2.8 convolution_bitcast_fusion
  320.2 0.2 copy.20
  320.4 6.1 fusion.3
  326.5 6.1 fusion
  332.6 23.3 %scatter_custom_fusion = f32[1024,256]{1,0:T(8,128)S(1)} fusion(s32[4096]{0:T(1024)S(1)} %get-tuple-element.12, f32[4096,256]{1,0:T(8,128)} %fusion.3, f32[]{:T(128)} %constant.13.clone.1), kind=kCustom, calls=%fused_computation.27 | custom fusion | flops 1048576 | bytes 1049088 | tf_op jit(solution)/shard_map/scatter-add | solution.py:50
  355.9 23.1 %scatter_custom_fusion.1 = f32[1024,256]{1,0:T(8,128)S(1)} fusion(s32[4096]{0:T(1024)S(1)} %get-tuple-element.11, f32[4096,256]{1,0:T(8,128)} %fusion, f32[]{:T(128)} %constant.13.clone.1), kind=kCustom, calls=%fused_computation.25 | custom fusion | flops 1048576 | bytes 1049088 | tf_op jit(solution)/shard_map/scatter-add | solution.py:50
  379.0 7.3 %scatter_custom_fusion.2 = f32[1024,256]{1,0:T(8,128)} fusion(s32[1024]{0:T(1024)} %param.7, f32[1024,256]{1,0:T(8,128)S(1)} %scatter_custom_fusion, f32[1024,256]{1,0:T(8,128)S(1)} %scatter_custom_fusion.1, f32[]{:T(128)} %constant.13.clone.1), kind=kCustom, calls=%fused_computation.18 | custom fusion | flops 524288 | bytes 3146240 | tf_op jit(solution)/shard_map/scatter-add | solution.py:51
  386.3 0.0 reduce-scatter.2.cloned.1.call-update
  386.3 28.8 %scatter_custom_fusion.3 = f32[1024]{0:T(1024)S(1)} fusion(s32[4096]{0:T(1024)S(1)} %get-tuple-element.12, f32[4096]{0:T(1024)S(1)} %broadcast.36, f32[]{:T(128)} %constant.13.clone.1), kind=kCustom, calls=%fused_computation.61 | custom fusion | flops 4096 | bytes 4100 | tf_op jit(solution)/shard_map/scatter-add | solution.py:46
  415.1 28.8 %scatter_custom_fusion.4 = f32[1024]{0:T(1024)S(1)} fusion(s32[4096]{0:T(1024)S(1)} %get-tuple-element.11, f32[4096]{0:T(1024)S(1)} %broadcast.36, f32[]{:T(128)} %constant.13.clone.1), kind=kCustom, calls=%fused_computation.59 | custom fusion | flops 4096 | bytes 4100 | tf_op jit(solution)/shard_map/scatter-add | solution.py:46
  443.9 7.8 %scatter_custom_fusion.5 = f32[1024]{0:T(1024)S(1)} fusion(s32[1024]{0:T(1024)} %param.7, f32[1024]{0:T(1024)S(1)} %add.67, f32[]{:T(128)} %constant.13.clone.1), kind=kCustom, calls=%fused_computation.57 | custom fusion | flops 1024 | bytes 4608 | tf_op jit(solution)/shard_map/scatter-add | solution.py:52
  451.7 1.3 dynamic-slice
  453.6 69.6 %all-reduce = f32[1024]{0:T(1024)S(1)} all-reduce(f32[1024]{0:T(1024)S(1)} %scatter_custom_fusion.5), channel_id=3, replica_groups=mesh['chan'=32,'freq'=16] {'chan'}, use_global_device_ids=true, to_apply=%region_10.11.clone | all-reduce | flops 1024 | bytes 8192
  523.2 0.1 fusion.37
  523.2 12.4 %reduce-scatter.2.cloned.1.call-done = f32[32,256]{1,0:T(8,128)} async-done(((f32[1024,256]{1,0:T(8,128)}), f32[32,256]{1,0:T(8,128)}) %reduce-scatter.2.cloned.1.call-update) | async-done | bytes 32784 | tf_op jit(solution)/shard_map/reduce_scatter | solution.py:54
  535.6 93.4 %psum.23 = f32[32,256]{1,0:T(8,128)S(1)} all-reduce(f32[32,256]{1,0:T(8,128)} %reduce-scatter.2.cloned.1.call-done), channel_id=1, replica_groups=mesh['chan'=32,'freq'=16] {'freq'}, use_global_device_ids=true, to_apply=%region_6.7 | all-reduce | flops 8192 | bytes 65536 | tf_op jit(solution)/shard_map/psum | solution.py:57
  629.0 0.7 broadcast_divide_fusion
  (6 shorter events, 0.0 us)
Async XLA Ops:
  6.5 1.2 copy-start
  6.5 5.0 copy-start.4
  6.5 294.1 %all-reduce.4.cloned.1.call-start = ((), (), s32[]{:S(2)}) async-start(), calls=%async_computation.2 | async-start | bytes 1966080 | tf_op jit(solution)/shard_map/psum | solution.py:43
  11.4 524.2 %reduce-scatter.2.cloned.1.call-start = ((), (), s32[]{:S(2)}) async-start(), calls=%async_computation.1 | async-start | bytes 1081344 | tf_op jit(solution)/shard_map/reduce_scatter | solution.py:54
  300.6 2.3 copy-start.2
  309.7 0.9 copy-start.3
  309.7 1.2 copy-start.1
Sparse Core Ops, SparseCore 0:
  11.6 289.0 all-reduce.3
  386.4 149.1 reduce-scatter.1
where the time goes:
time: 637 us
  waiting for transfers between devices  301 us (47%)
  blocking collectives  163 us (26%)
  other arithmetic  125 us (20%)
  matrix products  19.8 us (3%)
  between operations  14.2 us (2%)
  local copies, waits for them, and re-layouts  13.6 us (2%)
    psum x1, waiting for transfers between devices, body(): lax.psum(picked(spectra, src_ids[step_no]).astype(jnp.bfloat16), 'chan')  289 us
    psum x1, blocking collectives, body(): totals = lax.psum(owned, 'freq')  93.4 us
    unnamed x1, blocking collectives  69.6 us
    scatter-add x2, other arithmetic, body(): jax.ops.segment_sum(jnp.ones((bin_ids.shape[0],), jnp.float32), bin_ids,...  57.6 us
    scatter-add x2, other arithmetic, body(): jax.ops.segment_sum(traces, bin_ids, num_segments=bin_total)  46.4 us
  transfers between devices with their start and end apart: 2, of which 2 were waited for; matrix products, arithmetic and copies ran while one was open for 11% of the time, Pallas kernels for 0%

commit v1 on v0

--- a/solution.py
+++ b/solution.py
@@ -40,7 +40,9 @@
     counts = jnp.zeros((bin_total,), jnp.float32)
     summed = jnp.zeros((bin_total, NLAG), jnp.float32)
     for step_no in range(steps):
-        source = lax.psum(picked(spectra, src_ids[step_no]).astype(jnp.bfloat16), "chan")
+        source = jnp.sum(
+            lax.all_gather(picked(spectra, src_ids[step_no]).astype(jnp.bfloat16), "chan"), axis=0
+        )
         crossed = cross_terms(source, spectra)
         bin_ids = pair_bin[step_no].reshape(-1)
         counts = counts + jax.ops.segment_sum(

time: 637 us -> 561 us (0.88)
  waiting for transfers between devices: 301 us -> 206 us
  other arithmetic: 125 us -> 141 us
    psum x1 -> x0, waiting for transfers between devices: 289 us -> none  [body(): lax.psum(picked(spectra, src_ids[step_no]).astype(jnp.bfloat16), 'chan')]
    all_gather x0 -> x2, waiting for transfers between devices: none -> 194 us  [body(): lax.all_gather(picked(spectra, src_ids[step_no]).astype(jnp.bfloat16), 'c...]
    reduce_sum x0 -> x2, other arithmetic: none -> 17.9 us  [body(): jnp.sum(lax.all_gather(picked(spectra, src_ids[step_no]).astype(jnp.bfloa...]
  transfers between devices with their start and end apart: 2 -> 3, of which waited for: 2 -> 3; matrix products, arithmetic and copies ran while one was open for 11% -> 14% of each run, Pallas kernels for 0% -> 0%
where the time goes in v1:
time: 561 us; the launch traced here: 560 us
  waiting for transfers between devices  206 us (37%)
  blocking collectives  165 us (29%)
  other arithmetic  141 us (25%)
  matrix products  19.8 us (4%)
  between operations  13.9 us (2%)
  local copies, waits for them, and re-layouts  13.6 us (2%)
    all_gather x2, waiting for transfers between devices, body(): lax.all_gather(picked(spectra, src_ids[step_no]).astype(jnp.bfloat16), 'c...  194 us
    psum x1, blocking collectives, body(): totals = lax.psum(owned, 'freq')  93.2 us
    unnamed x1, blocking collectives  72.2 us
    scatter-add x2, other arithmetic, body(): jax.ops.segment_sum(jnp.ones((bin_ids.shape[0],), jnp.float32), bin_ids,...  57.8 us
    scatter-add x2, other arithmetic, body(): jax.ops.segment_sum(traces, bin_ids, num_segments=bin_total)  46.2 us
    reduce_sum x2, other arithmetic, body(): jnp.sum(lax.all_gather(picked(spectra, src_ids[step_no]).astype(jnp.bfloa...  17.9 us
    dot_general x2, matrix products, body(): traces = jnp.dot(crossed, lag_table, precision=lax.Precision.HIGHEST)  12.2 us
    reduce_scatter x1, waiting for transfers between devices, body(): lax.psum_scatter(summed, 'chan', scatter_dimension=0, tiled=True)  11.8 us
  transfers between devices with their start and end apart: 3, of which 3 were waited for; matrix products, arithmetic and copies ran while one was open for 14% of the time, Pallas kernels for 0%

profile of v1, /device:TPU:128, one launch (start us, length us, event | category | flops | bytes accessed | tf_op | source)
XLA Modules:
  0.0 560.2 jit_solution(1521135735779695859)
XLA Ops:
  6.5 0.0 copy-start
  6.5 0.0 copy-start.4
  6.5 0.0 all-gather.7.cloned.1.call-start
  6.5 0.8 slice_bitcast_fusion.2
  7.3 0.4 copy-done
  7.8 1.8 fusion.7
  9.6 0.0 all-gather.7.cloned.1.call-update
  9.6 0.0 all-gather.5.cloned.1.call-start
  9.7 1.8 fusion.6
  11.5 0.0 all-gather.5.cloned.1.call-update
  11.5 0.0 reduce-scatter.2.cloned.1.call-start
  11.6 0.0 copy-done.4
  11.6 0.3 fusion.22
  12.0 100.4 %all-gather.7.cloned.1.call-done = bf16[64,30,64,32]{2,3,1,0:T(8,128)(2,1)} async-done(((bf16[2,30,64,32]{2,3,1,0:T(8,128)(2,1)}), bf16[64,30,64,32]{2,3,1,0:T(8,128)(2,1)}) %all-gather.7.cloned.1.call-update) | async-done | bytes 7864336 | tf_op jit(solution)/shard_map/all_gather | solution.py:44
  112.4 9.0 %reduce_sum.25 = bf16[2,30,64,32]{2,3,1,0:T(8,128)(2,1)S(1)} reduce(bf16[32,2,30,64,32]{3,4,2,1,0:T(8,128)(2,1)} %bitcast.63, bf16[]{:T(256)} %constant.35.clone.1), dimensions={0}, to_apply=%region_2.3 | reduce | flops 3809280 | bytes 8110082 | tf_op jit(solution)/shard_map/reduce_sum | solution.py:43
  121.3 93.7 %all-gather.5.cloned.1.call-done = bf16[64,30,64,32]{2,3,1,0:T(8,128)(2,1)} async-done(((bf16[2,30,64,32]{2,3,1,0:T(8,128)(2,1)}), bf16[64,30,64,32]{2,3,1,0:T(8,128)(2,1)}) %all-gather.5.cloned.1.call-update) | async-done | bytes 7864336 | tf_op jit(solution)/shard_map/all_gather | solution.py:44
  215.1 9.0 %reduce_sum.24 = bf16[2,30,64,32]{2,3,1,0:T(8,128)(2,1)S(1)} reduce(bf16[32,2,30,64,32]{3,4,2,1,0:T(8,128)(2,1)} %bitcast.64, bf16[]{:T(256)} %constant.35.clone.1), dimensions={0}, to_apply=%region_0.1 | reduce | flops 3809280 | bytes 8110082 | tf_op jit(solution)/shard_map/reduce_sum | solution.py:43
  224.0 0.0 copy-start.1
  224.0 0.8 slice_negate_fusion.1
  224.9 0.1 maximum_bitcast_fusion.1
  225.0 0.0 copy-done.1
  225.0 1.2 pad_maximum_fusion.1
  226.2 4.5 copy.18
  230.7 1.2 convolution_bitcast_fusion
  231.9 0.0 copy-start.3
  231.9 0.2 copy.20
  232.1 0.7 copy-done.3
  232.8 0.1 maximum_bitcast_fusion
  232.9 0.1 copy-done.2
  233.0 1.2 pad_maximum_fusion
  234.2 5.3 copy.15
  239.5 2.8 convolution_bitcast_fusion.1
  242.3 0.2 copy.17
  242.5 6.1 %fusion.3 = f32[4096,256]{1,0:T(8,128)} fusion(f32[16,8,32,128]{3,2,1,0:T(8,128)S(1)} %bitcast.66, f32[64,256]{1,0:T(8,128)S(1)} %get-tuple-element.12, f32[64,256]{1,0:T(8,128)S(1)} %get-tuple-element.11), kind=kOutput, calls=%fused_computation.9 | convolution fusion | flops 1610678272 | bytes 6422528 | tf_op jit(solution)/shard_map/dot_general | solution.py:51
  248.6 6.1 %fusion = f32[4096,256]{1,0:T(8,128)} fusion(f32[16,8,32,128]{3,2,1,0:T(8,128)S(1)} %bitcast.65, f32[64,256]{1,0:T(8,128)S(1)} %get-tuple-element.12, f32[64,256]{1,0:T(8,128)S(1)} %get-tuple-element.11), kind=kOutput, calls=%fused_computation.6 | convolution fusion | flops 1610678272 | bytes 6422528 | tf_op jit(solution)/shard_map/dot_general | solution.py:51
  254.7 23.1 %scatter_custom_fusion = f32[1024,256]{1,0:T(8,128)S(1)} fusion(s32[4096]{0:T(1024)S(1)} %get-tuple-element.10, f32[4096,256]{1,0:T(8,128)} %fusion.3, f32[]{:T(128)} %constant.14.clone.1), kind=kCustom, calls=%fused_computation.27 | custom fusion | flops 1048576 | bytes 1049088 | tf_op jit(solution)/shard_map/scatter-add | solution.py:52
  277.8 23.1 %scatter_custom_fusion.1 = f32[1024,256]{1,0:T(8,128)S(1)} fusion(s32[4096]{0:T(1024)S(1)} %get-tuple-element.9, f32[4096,256]{1,0:T(8,128)} %fusion, f32[]{:T(128)} %constant.14.clone.1), kind=kCustom, calls=%fused_computation.25 | custom fusion | flops 1048576 | bytes 1049088 | tf_op jit(solution)/shard_map/scatter-add | solution.py:52
  300.9 7.3 %scatter_custom_fusion.2 = f32[1024,256]{1,0:T(8,128)} fusion(s32[1024]{0:T(1024)} %param.7, f32[1024,256]{1,0:T(8,128)S(1)} %scatter_custom_fusion, f32[1024,256]{1,0:T(8,128)S(1)} %scatter_custom_fusion.1, f32[]{:T(128)} %constant.14.clone.1), kind=kCustom, calls=%fused_computation.18 | custom fusion | flops 524288 | bytes 3146240 | tf_op jit(solution)/shard_map/scatter-add | solution.py:53
  308.2 0.0 reduce-scatter.2.cloned.1.call-update
  308.2 28.8 %scatter_custom_fusion.4 = f32[1024]{0:T(1024)S(1)} fusion(s32[4096]{0:T(1024)S(1)} %get-tuple-element.9, f32[4096]{0:T(1024)S(1)} %broadcast.36, f32[]{:T(128)} %constant.14.clone.1), kind=kCustom, calls=%fused_computation.59 | custom fusion | flops 4096 | bytes 4100 | tf_op jit(solution)/shard_map/scatter-add | solution.py:48
  337.0 29.0 %scatter_custom_fusion.3 = f32[1024]{0:T(1024)S(1)} fusion(s32[4096]{0:T(1024)S(1)} %get-tuple-element.10, f32[4096]{0:T(1024)S(1)} %broadcast.36, f32[]{:T(128)} %constant.14.clone.1), kind=kCustom, calls=%fused_computation.61 | custom fusion | flops 4096 | bytes 4100 | tf_op jit(solution)/shard_map/scatter-add | solution.py:48
  366.1 7.8 %scatter_custom_fusion.5 = f32[1024]{0:T(1024)S(1)} fusion(s32[1024]{0:T(1024)} %param.7, f32[1024]{0:T(1024)S(1)} %add.63, f32[]{:T(128)} %constant.14.clone.1), kind=kCustom, calls=%fused_computation.57 | custom fusion | flops 1024 | bytes 4608 | tf_op jit(solution)/shard_map/scatter-add | solution.py:54
  373.8 1.3 dynamic-slice
  375.7 72.2 %all-reduce = f32[1024]{0:T(1024)S(1)} all-reduce(f32[1024]{0:T(1024)S(1)} %scatter_custom_fusion.5), channel_id=5, replica_groups=mesh['chan'=32,'freq'=16] {'chan'}, use_global_device_ids=true, to_apply=%region_10.11.clone | all-reduce | flops 1024 | bytes 8192
  447.9 0.1 fusion.37
  448.0 11.8 %reduce-scatter.2.cloned.1.call-done = f32[32,256]{1,0:T(8,128)} async-done(((f32[1024,256]{1,0:T(8,128)}), f32[32,256]{1,0:T(8,128)}) %reduce-scatter.2.cloned.1.call-update) | async-done | bytes 32784 | tf_op jit(solution)/shard_map/reduce_scatter | solution.py:56
  459.7 93.2 %psum.7 = f32[32,256]{1,0:T(8,128)S(1)} all-reduce(f32[32,256]{1,0:T(8,128)} %reduce-scatter.2.cloned.1.call-done), channel_id=1, replica_groups=mesh['chan'=32,'freq'=16] {'freq'}, use_global_device_ids=true, to_apply=%region_6.7 | all-reduce | flops 8192 | bytes 65536 | tf_op jit(solution)/shard_map/psum | solution.py:59
  553.0 0.7 broadcast_divide_fusion
  (8 shorter events, 0.1 us)
Async XLA Ops:
  6.5 1.2 copy-start
  6.5 5.1 copy-start.4
  6.5 105.8 %all-gather.7.cloned.1.call-start = ((), (), s32[]{:S(2)}) async-start(), calls=%async_computation.3 | async-start | bytes 16220160 | tf_op jit(solution)/shard_map/all_gather | solution.py:44
  9.6 205.5 %all-gather.5.cloned.1.call-start = ((), (), s32[]{:S(2)}) async-start(), calls=%async_computation.2 | async-start | bytes 16220160 | tf_op jit(solution)/shard_map/all_gather | solution.py:44
  11.5 448.2 %reduce-scatter.2.cloned.1.call-start = ((), (), s32[]{:S(2)}) async-start(), calls=%async_computation.1 | async-start | bytes 1081344 | tf_op jit(solution)/shard_map/reduce_scatter | solution.py:56
  224.0 1.0 copy-start.1
  231.9 0.9 copy-start.3
  231.9 1.2 copy-start.2
Sparse Core Ops, SparseCore 0:
  9.7 102.6 all-gather.6
  114.5 100.4 all-gather.4
  308.4 151.3 reduce-scatter.1
